TPU v7x, 32 devices: a whole 2x2x4 slice. The times are simulated.
32 devices in a mesh: date: 2 (over y), slab: 16 (over z, x, core).
Axes of the slice: x: 2, y: 2, z: 4, core: 2. Of those that a mesh axis runs over, the one named last changes fastest.
Arguments:
- pressure: float32 [16, 12288], P('slab', 'date'), parts along dimension 1, may hold values from -6 to 6
- density: float32 [16, 12288], P('slab', 'date'), parts along dimension 1, may hold values from -6 to 6
- vertical_wind: float32 [16, 12288], P('slab', 'date'), parts along dimension 1, may hold values from -6 to 6
- horizontal_wind: float32 [2, 16, 12288], P(None, 'slab', 'date'), parts along dimension 2, may hold values from -6 to 6
- metric_terms: float32 [2, 6144], replicated, may hold values from 0.25 to 1
- neighbors: int32 [4, 6144], replicated, may hold values from 0 to 6143, as said below
- level_order: int32 [16], replicated, may hold values from 0 to 15, each once
- stiffness: float32 [16], replicated, may hold values from 0.2 to 5
- coupling: float32 [16], replicated, may hold values from 0.2 to 1
- weight_one: bfloat16 [64, 512], P('slab'), may hold values from -0.75 to 0.75
- weight_two: bfloat16 [512, 512], P('slab'), may hold values from -0.25 to 0.25
- weight_three: bfloat16 [512, 16], P('slab'), may hold values from -0.25 to 0.25
- pressure_adjoint: float32 [16, 12288], P('slab', 'date'), parts along dimension 1, may hold values from -6 to 6
- wind_adjoint: float32 [16, 12288], P('slab', 'date'), parts along dimension 1, may hold values from -6 to 6
Outputs:
- pressure_new: float32 [16, 12288], P('slab', 'date'), parts along dimension 1
- wind_new: float32 [16, 12288], P('slab', 'date'), parts along dimension 1
- pressure_grad: float32 [16, 12288], P('slab', 'date'), parts along dimension 1
- first_grad: float32 [128, 512], P(('date', 'slab')), parts along dimension 0
- second_grad: float32 [1024, 512], P(('date', 'slab')), parts along dimension 0
- third_grad: float32 [1024, 16], P(('date', 'slab')), parts along dimension 0
There are 2 independent parts, one for each index of `date`. A program takes and returns all parts, laid end to end along the dimension named above; an argument that names none is the same for every part. Nothing has to cross between parts.
Inputs may be any that keep to these rules, and one draw needn't show every extreme that they name: `neighbors`: the columns are the cells of a 8 x 768 grid stored in some order; rows 0, 1, 2, 3 give the stored positions of a column's east, west, north and south neighbours, and the column itself where the grid's edge lies on that side. `level_order`: each level appears once.
All inputs are finite; a program needn't handle non-finite values.
Results may differ from a plain program's by a relative error of at most 0.0075.
Values may be sent and summed in bfloat16 or wider, within the bound.
No kernel may reach another device: no remote copies, remote signals or barrier semaphores. Data moves between devices by JAX's collectives and lax.ppermute only.
A program may use at most 128 MiB of HBM per device.

v0:
```python
import math
import jax
import jax.numpy as jnp
from jax import lax
from jax.sharding import PartitionSpec as P


def lower_diff(field):
    return jnp.concatenate([field[1:] - field[:-1], -field[-1:]], axis=0)


def upper_diff(field):
    return jnp.concatenate([jnp.zeros_like(field[:1]), field[:-1]], axis=0) - field


def level_inverse(stiffness):
    below = jnp.concatenate([jnp.zeros((1,), jnp.float32), stiffness[:-1]])
    matrix = (
        jnp.diag(1.0 + stiffness + below)
        - jnp.diag(stiffness[:-1], 1)
        - jnp.diag(stiffness[:-1], -1)
    )
    factor = jnp.linalg.cholesky(matrix)
    identity = jnp.eye(stiffness.shape[0], dtype=jnp.float32)
    return jax.scipy.linalg.cho_solve((factor, True), identity)


def apply_inverse(inverse_matrix, rhs):
    return jnp.dot(
        inverse_matrix, rhs, precision=lax.Precision.HIGHEST, preferred_element_type=jnp.float32
    )


def contract_first(left, right):
    return lax.dot_general(
        left, right, (((0,), (0,)), ((), ())), preferred_element_type=jnp.float32
    )


def contract_last(left, right):
    return lax.dot_general(
        left, right, (((1,), (1,)), ((), ())), preferred_element_type=jnp.float32
    )


def body(
    pressure,
    density,
    vertical_wind,
    horizontal_wind,
    metric_terms,
    neighbors,
    level_order,
    stiffness,
    coupling,
    weight_one,
    weight_two,
    weight_three,
    pressure_adjoint,
    wind_adjoint,
):
    east = jnp.take(horizontal_wind[0], neighbors[0], axis=1)
    west = jnp.take(horizontal_wind[0], neighbors[1], axis=1)
    north = jnp.take(horizontal_wind[1], neighbors[2], axis=1)
    south = jnp.take(horizontal_wind[1], neighbors[3], axis=1)
    diverg = metric_terms[0] * (east - west) + metric_terms[1] * (north - south)
    star = pressure - diverg
    inverse = jnp.argsort(level_order)
    scale = 1.0 / math.sqrt(neighbors.shape[1])
    forward_raw = lax.all_to_all(
        jnp.stack([star, density, vertical_wind, diverg]).astype(jnp.bfloat16),
        "slab",
        split_axis=2,
        concat_axis=1,
        tiled=True,
    ).astype(jnp.float32)
    full_one, full_two, full_three = (
        lax.all_gather(weight_one, "slab", axis=0, tiled=True),
        lax.all_gather(weight_two, "slab", axis=0, tiled=True),
        lax.all_gather(weight_three, "slab", axis=0, tiled=True),
    )
    forward_part = jnp.take(forward_raw, inverse, axis=1)
    levels = forward_part.shape[1]
    width = forward_part.shape[2]
    couple = coupling[:, None]
    column_input = forward_part.reshape(4 * levels, width).astype(jnp.bfloat16)
    pre_one = contract_first(full_one, column_input)
    tanh_one = jnp.tanh(pre_one)
    act_one = tanh_one.astype(jnp.bfloat16)
    pre_two = contract_first(full_two, act_one)
    tanh_two = jnp.tanh(pre_two)
    act_two = tanh_two.astype(jnp.bfloat16)
    heating = contract_first(full_three, act_two)
    star_column = forward_part[0]
    rhs = forward_part[2] - couple * lower_diff(star_column) - 0.5 * forward_part[1] + heating
    inverse_matrix = level_inverse(stiffness)
    wind_next = apply_inverse(inverse_matrix, rhs)
    press_next = star_column + upper_diff(couple * wind_next)
    forward_slabs = lax.all_to_all(
        jnp.take(jnp.stack([press_next, wind_next]), level_order, axis=1).astype(jnp.bfloat16),
        "slab",
        split_axis=1,
        concat_axis=2,
        tiled=True,
    ).astype(jnp.float32)
    adjoint_raw = lax.all_to_all(
        jnp.stack([pressure_adjoint, wind_adjoint]), "slab", split_axis=2, concat_axis=1, tiled=True
    )
    adjoint_part = jnp.take(adjoint_raw, inverse, axis=1)
    wind_grad = adjoint_part[1] + couple * lower_diff(adjoint_part[0])
    rhs_grad = apply_inverse(inverse_matrix, wind_grad)
    star_grad = adjoint_part[0] - upper_diff(couple * rhs_grad)
    heat_grad = rhs_grad.astype(jnp.bfloat16)
    local_three = contract_last(act_two, heat_grad) * scale
    back_two = jnp.dot(full_three, heat_grad, preferred_element_type=jnp.float32)
    pre_two_grad = (back_two * (1.0 - tanh_two * tanh_two)).astype(jnp.bfloat16)
    local_two = contract_last(act_one, pre_two_grad) * scale
    back_one = jnp.dot(full_two, pre_two_grad, preferred_element_type=jnp.float32)
    pre_one_grad = (back_one * (1.0 - tanh_one * tanh_one)).astype(jnp.bfloat16)
    local_one = contract_last(column_input, pre_one_grad) * scale
    first_grad, second_grad, third_grad = (
        lax.psum_scatter(local_one, "slab", scatter_dimension=0, tiled=True),
        lax.psum_scatter(local_two, "slab", scatter_dimension=0, tiled=True),
        lax.psum_scatter(local_three, "slab", scatter_dimension=0, tiled=True),
    )
    input_grad = jnp.dot(full_one, pre_one_grad, preferred_element_type=jnp.float32)
    star_grad = star_grad + input_grad[:levels]
    stored_grad = jnp.take(star_grad, level_order, axis=0)
    pressure_new = forward_slabs[0]
    wind_new = forward_slabs[1]
    pressure_grad = lax.all_to_all(
        stored_grad[None].astype(jnp.bfloat16), "slab", split_axis=1, concat_axis=2, tiled=True
    ).astype(jnp.float32)[0]
    return (pressure_new, wind_new, pressure_grad, first_grad, second_grad, third_grad)


def solution(mesh):
    in_specs = (
        P("slab", "date"),
        P("slab", "date"),
        P("slab", "date"),
        P(None, "slab", "date"),
        P(),
        P(),
        P(),
        P(),
        P(),
        P("slab", None),
        P("slab", None),
        P("slab", None),
        P("slab", "date"),
        P("slab", "date"),
    )
    out_specs = (
        P("slab", "date"),
        P("slab", "date"),
        P("slab", "date"),
        P(("date", "slab"), None),
        P(("date", "slab"), None),
        P(("date", "slab"), None),
    )
    return jax.shard_map(body, mesh=mesh, in_specs=in_specs, out_specs=out_specs, check_vma=False)
```

profile of v0, /device:TPU:0, one launch (start us, length us, event | category | flops | bytes accessed | tf_op | source)
XLA Modules:
  0.0 540.4 jit_solution(8033137742579381662)
XLA Ops:
  7.2 1.2 fusion.38
  8.4 0.8 fusion.39
  9.1 34.3 %gather_fusion.4 = f32[6144]{0:T(1024)S(1)} fusion(f32[6144]{0:T(1024)S(1)} %bitcast.140, s32[6144]{0:T(1024)S(1)} %fusion.25), kind=kCustom, calls=%fused_computation.3.clone | custom fusion | bytes 73728 | tf_op jit(solution)/shard_map/jit(_take)/gather | solution.py:64
  43.5 34.3 %gather_fusion.5 = f32[6144]{0:T(1024)S(1)} fusion(f32[6144]{0:T(1024)S(1)} %bitcast.141, s32[6144]{0:T(1024)S(1)} %fusion.26), kind=kCustom, calls=%fused_computation.4.clone | custom fusion | bytes 73728 | tf_op jit(solution)/shard_map/jit(_take)/gather | solution.py:65
  77.8 34.3 %gather_fusion.2 = f32[6144]{0:T(1024)S(1)} fusion(f32[6144]{0:T(1024)S(1)} %bitcast.138, s32[6144]{0:T(1024)S(1)} %fusion.23), kind=kCustom, calls=%fused_computation.clone | custom fusion | bytes 73728 | tf_op jit(solution)/shard_map/jit(_take)/gather | solution.py:62
  112.2 34.3 %gather_fusion.3 = f32[6144]{0:T(1024)S(1)} fusion(f32[6144]{0:T(1024)S(1)} %bitcast.139, s32[6144]{0:T(1024)S(1)} %fusion.24), kind=kCustom, calls=%fused_computation.2.clone | custom fusion | bytes 73728 | tf_op jit(solution)/shard_map/jit(_take)/gather | solution.py:63
  146.7 0.2 pad_maximum_fusion
  146.9 4.0 copy.50
  150.9 0.5 broadcast.246
  151.5 34.5 %reduce.6 = bf16[6144,4]{1,0:T(8,128)(2,1)} reduce(bf16[6144,1,4]{2,1,0:T(2,128)(2,1)S(1)} %bitcast.142, bf16[]{:T(256)} %broadcast.246), dimensions={1}, to_apply=%bitcast.107.reduce_sub_computation | reduce | bytes 98306
  186.0 4.4 reshape.350
  190.4 7.4 %all-to-all-start = ((bf16[16,2,768]{2,1,0:T(2,128)(2,1)}), bf16[16,2,768]{2,1,0:T(2,128)(2,1)S(1)}, u32[]{:S(2)}, u32[]{:S(2)}) async-start(bf16[16,2,768]{2,1,0:T(2,128)(2,1)} %reshape.350), calls=%async_computation | async-start | bytes 98304 | tf_op jit(solution)/shard_map/all_to_all | solution.py:70
  197.8 1.2 sort.17
  199.2 21.9 %all-gather = bf16[16,4,512]{2,1,0:T(4,128)(2,1)S(1)} all-gather(bf16[1,4,512]{2,1,0:T(4,128)(2,1)S(1)} %bitcast.168), channel_id=1, replica_groups=mesh['date'=2,'slab'=16] {'slab'}, dimensions={0}, use_global_device_ids=true | all-gather | bytes 69632 | tf_op jit(solution)/shard_map/all_gather | solution.py:78
  221.1 20.3 %all_gather.10 = bf16[512,512]{1,0:T(8,128)(2,1)} all-gather(bf16[32,512]{1,0:T(8,128)(2,1)S(1)} %copy-done.2), channel_id=1, replica_groups=mesh['date'=2,'slab'=16] {'slab'}, dimensions={0}, use_global_device_ids=true | all-gather | bytes 557056 | tf_op jit(solution)/shard_map/all_gather | solution.py:79
  241.4 19.3 %all-gather.1 = bf16[16,32,16]{1,2,0:T(8,128)(2,1)S(1)} all-gather(bf16[1,32,16]{1,2,0:T(8,128)(2,1)S(1)} %bitcast.169), channel_id=1, replica_groups=mesh['date'=2,'slab'=16] {'slab'}, dimensions={0}, use_global_device_ids=true | all-gather | bytes 17408 | tf_op jit(solution)/shard_map/all_gather | solution.py:80
  261.0 1.4 cholesky.17
  262.5 0.6 compare_reduce_fusion
  263.1 0.6 fusion.28
  263.8 1.2 custom-call.10
  265.0 0.2 fusion.31
  265.2 0.1 fusion.29
  265.4 3.3 copy.56
  268.7 0.5 broadcast.247
  269.2 28.4 %reduce.7 = f32[6144,2]{1,0:T(8,128)} reduce(f32[6144,1,2]{2,1,0:T(1,128)S(1)} %bitcast.143, f32[]{:T(128)} %broadcast.247), dimensions={1}, to_apply=%bitcast.109.reduce_sub_computation | reduce | bytes 98308
  297.6 4.3 reshape.352
  302.0 3.5 all-to-all-start.2
  305.5 0.3 reduce-scatter.7.cloned.1.call-start
  305.7 4.0 reshape.351
  309.7 2.9 copy.51
  312.7 0.6 gather_fusion
  313.4 0.8 reduce.8
  314.2 4.5 reshape.353
  318.7 1.2 copy.58
  319.9 0.6 gather_fusion.7
  320.7 0.3 convolution_tanh_fusion.1
  321.0 1.4 convolution_tanh_fusion
  322.4 0.2 fusion.2
  322.7 0.2 fusion.41
  322.9 0.2 broadcast_multiply_fusion
  323.1 0.2 convolution_multiply_fusion.4
  323.3 0.3 fusion.1
  323.6 0.8 copy.63
  324.5 0.4 fusion
  324.9 0.8 convolution_multiply_fusion.3
  325.8 1.4 convolution_multiply_fusion
  327.3 0.3 convolution_bitcast_fusion
  327.6 0.6 gather_fusion.1
  328.3 0.7 reduce.9
  329.0 0.7 reshape.354
  329.7 6.0 %all-to-all-start.3 = ((bf16[16,2,192]{2,1,0:T(2,128)(2,1)}), bf16[16,2,192]{2,1,0:T(2,128)(2,1)S(1)}, u32[]{:S(2)}, u32[]{:S(2)}) async-start(bf16[16,2,192]{2,1,0:T(2,128)(2,1)} %reshape.354), calls=%async_computation.3 | async-start | bytes 32768 | tf_op jit(solution)/shard_map/all_to_all | solution.py:131
  335.7 0.6 gather_fusion.6
  336.3 0.7 bitcast_convert_fusion
  337.0 5.1 all-to-all-done.3
  342.2 3.5 all-to-all-start.1
  345.7 0.6 dynamic-slice
  347.0 0.6 convert.31
  347.7 4.5 all-to-all-done.1
  352.2 0.7 fusion.40
  352.8 28.3 %reduce-scatter.7.cloned.1.call-done = f32[32,16]{1,0:T(8,128)} async-done(((f32[512,16]{1,0:T(8,128)}), f32[32,16]{1,0:T(8,128)}) %reduce-scatter.7.cloned.1.call-update) | async-done | bytes 2064
  381.1 1.4 copy.64
  382.5 88.1 %all-reduce.6.cloned.1.call-done = f32[64,512]{1,0:T(8,128)} async-done(((f32[64,512]{1,0:T(8,128)}), f32[64,512]{1,0:T(8,128)}) %all-reduce.6.cloned.1.call-update) | async-done | bytes 131088
  470.6 1.3 constant_dynamic-slice_fusion
  472.0 61.9 %reduce-scatter.5.cloned.1.call-done = f32[32,512]{1,0:T(8,128)} async-done(((f32[512,512]{1,0:T(8,128)}), f32[32,512]{1,0:T(8,128)}) %reduce-scatter.5.cloned.1.call-update) | async-done | bytes 65552 | tf_op jit(solution)/shard_map/reduce_scatter | solution.py:123
  (81 shorter events, 1.5 us)
Async XLA Ops:
  112.1 34.4 %copy-start.4 = (f32[1,6144]{1,0:T(1,128)S(1)}, f32[1,6144]{1,0:T(1,128)}, u32[]{:S(2)}) copy-start(f32[1,6144]{1,0:T(1,128)} %param.19) | copy-start | bytes 73732
  112.1 34.4 %copy-start.1 = (f32[2,6144]{1,0:T(2,128)S(1)}, f32[2,6144]{1,0:T(2,128)}, u32[]{:S(2)}) copy-start(f32[2,6144]{1,0:T(2,128)} %param.22) | copy-start | bytes 147460
  112.1 34.4 %copy-start.3 = (f32[1,6144]{1,0:T(1,128)S(1)}, f32[1,6144]{1,0:T(1,128)}, u32[]{:S(2)}) copy-start(f32[1,6144]{1,0:T(1,128)} %param.18) | copy-start | bytes 73732
  112.1 34.5 %copy-start.5 = (f32[1,6144]{1,0:T(1,128)S(1)}, f32[1,6144]{1,0:T(1,128)}, u32[]{:S(2)}) copy-start(f32[1,6144]{1,0:T(1,128)} %param.20) | copy-start | bytes 73732
  151.4 46.3 %copy-start.13 = (s32[16]{0:T(128)S(1)}, s32[16]{0:T(128)}, u32[]{:S(2)}) copy-start(s32[16]{0:T(128)} %param.24) | copy-start | bytes 196
  151.5 47.7 %copy-start.8 = (bf16[4,512]{1,0:T(4,128)(2,1)S(1)}, bf16[4,512]{1,0:T(4,128)(2,1)}, u32[]{:S(2)}) copy-start(bf16[4,512]{1,0:T(4,128)(2,1)} %param.27) | copy-start | bytes 12292
  151.5 69.6 %copy-start.2 = (bf16[32,512]{1,0:T(8,128)(2,1)S(1)}, bf16[32,512]{1,0:T(8,128)(2,1)}, u32[]{:S(2)}) copy-start(bf16[32,512]{1,0:T(8,128)(2,1)} %param.28) | copy-start | bytes 98308
  151.5 89.9 %copy-start.9 = (bf16[32,16]{0,1:T(8,128)(2,1)S(1)}, bf16[32,16]{0,1:T(8,128)(2,1)}, u32[]{:S(2)}) copy-start(bf16[32,16]{0,1:T(8,128)(2,1)} %param.29) | copy-start | bytes 3076
  151.5 109.3 %copy-start.10 = (f32[16]{0:T(128)S(1)}, f32[16]{0:T(128)}, u32[]{:S(2)}) copy-start(f32[16]{0:T(128)} %param.25) | copy-start | bytes 196
  151.5 109.3 %copy-start.12 = (pred[16]{0:T(512)(128)(4,1)S(1)}, pred[16]{0:T(512)(128)(4,1)}, u32[]{:S(2)}) copy-start(pred[16]{0:T(512)(128)(4,1)} %constant.116.clone.1) | copy-start | bytes 52
  151.5 113.9 %copy-start.6 = (f32[1,6144]{1,0:T(1,128)S(1)}, f32[1,6144]{1,0:T(1,128)}, u32[]{:S(2)}) copy-start(f32[1,6144]{1,0:T(1,128)} %param.31) | copy-start | bytes 73732
  151.5 113.9 %copy-start.7 = (f32[1,6144]{1,0:T(1,128)S(1)}, f32[1,6144]{1,0:T(1,128)}, u32[]{:S(2)}) copy-start(f32[1,6144]{1,0:T(1,128)} %param.30) | copy-start | bytes 73732
  190.4 111.6 %all-to-all-start = ((bf16[16,2,768]{2,1,0:T(2,128)(2,1)}), bf16[16,2,768]{2,1,0:T(2,128)(2,1)S(1)}, u32[]{:S(2)}, u32[]{:S(2)}) async-start(bf16[16,2,768]{2,1,0:T(2,128)(2,1)} %reshape.350), calls=%async_computation | async-start | bytes 98304 | tf_op jit(solution)/shard_map/all_to_all | solution.py:70
  302.0 11.4 %all-to-all-start.2 = ((f32[16,1,768]{2,1,0:T(1,128)}), f32[16,1,768]{2,1,0:T(1,128)S(1)}, u32[]{:S(2)}, u32[]{:S(2)}) async-start(f32[16,1,768]{2,1,0:T(1,128)} %reshape.352), calls=%async_computation.2 | async-start | bytes 98304 | tf_op jit(solution)/shard_map/all_to_all | solution.py:106
  305.5 75.7 %reduce-scatter.7.cloned.1.call-start = ((), (), s32[]{:S(2)}) async-start(), calls=%async_computation.7 | async-start | bytes 278528
  318.7 3.7 copy-start.11
  320.7 3.8 copy-start
  324.4 146.2 %all-reduce.6.cloned.1.call-start = ((), (), s32[]{:S(2)}) async-start(), calls=%async_computation.8 | async-start | bytes 262144
  324.9 20.8 %copy-start.14 = (u32[32]{0:T(128)S(1)}, u32[32]{0:T(128)}, u32[]{:S(2)}) copy-start(u32[32]{0:T(128)} %constant.136) | copy-start | bytes 388
  325.8 208.2 %reduce-scatter.5.cloned.1.call-start = ((), (), s32[]{:S(2)}) async-start(), calls=%async_computation.6 | async-start | bytes 1114112 | tf_op jit(solution)/shard_map/reduce_scatter | solution.py:123
  329.7 12.5 %all-to-all-start.3 = ((bf16[16,2,192]{2,1,0:T(2,128)(2,1)}), bf16[16,2,192]{2,1,0:T(2,128)(2,1)S(1)}, u32[]{:S(2)}, u32[]{:S(2)}) async-start(bf16[16,2,192]{2,1,0:T(2,128)(2,1)} %reshape.354), calls=%async_computation.3 | async-start | bytes 32768 | tf_op jit(solution)/shard_map/all_to_all | solution.py:131
  342.2 10.0 %all-to-all-start.1 = ((bf16[2,16,384]{2,0,1:T(2,128)(2,1)}), bf16[2,16,384]{2,0,1:T(2,128)(2,1)S(1)}, u32[]{:S(2)}, u32[]{:S(2)}) async-start(bf16[2,16,384]{2,0,1:T(2,128)(2,1)} %bitcast_convert_fusion), calls=%async_computation.1 | async-start | bytes 49152 | tf_op jit(solution)/shard_map/all_to_all | solution.py:99
Sparse Core Ops, SparseCore 0:
  324.5 56.5 reduce-scatter.6
  384.6 86.0 all-reduce.5
  474.8 59.0 reduce-scatter.4
where the time goes:
time: 541 us; the launch traced here: 540 us
  waiting for transfers between devices  188 us (35%)
  local copies, waits for them, and re-layouts  177 us (33%)
  other arithmetic  72 us (13%)
  blocking collectives  61.4 us (11%)
  starting transfers between devices  20.7 us (4%)
  between operations  15 us (3%)
  matrix products  6.09 us (1%)
    unnamed x5, waiting for transfers between devices  116 us
    unnamed x3, other arithmetic  63.6 us
    reduce_scatter x1, waiting for transfers between devices, body(): lax.psum_scatter(local_two, 'slab', scatter_dimension=0, tiled=True)  61.9 us
    gather x1, local copies, waits for them, and re-layouts, body(): south = jnp.take(horizontal_wind[1], neighbors[3], axis=1)  34.3 us
    gather x1, local copies, waits for them, and re-layouts, body(): east = jnp.take(horizontal_wind[0], neighbors[0], axis=1)  34.3 us
    gather x1, local copies, waits for them, and re-layouts, body(): west = jnp.take(horizontal_wind[0], neighbors[1], axis=1)  34.3 us
    gather x1, local copies, waits for them, and re-layouts, body(): north = jnp.take(horizontal_wind[1], neighbors[2], axis=1)  34.3 us
    unnamed x44, local copies, waits for them, and re-layouts  23.4 us
  transfers between devices with their start and end apart: 7, of which 5 were waited for; matrix products, arithmetic and copies ran while one was open for 11% of the time, Pallas kernels for 0%

commit v1 on v0

--- a/solution.py
+++ b/solution.py
@@ -3,6 +3,27 @@
 import jax.numpy as jnp
 from jax import lax
 from jax.sharding import PartitionSpec as P
+
+
+def gather_around(array, axis, dim):
+    size, index, extent = (lax.axis_size(axis), lax.axis_index(axis), array.shape[dim])
+    ahead = [(i, (i + 1) % size) for i in range(size)]
+    left = [(i, (i - 1) % size) for i in range(size)]
+    whole = jnp.zeros((*array.shape[:dim], size * extent, *array.shape[dim + 1 :]), array.dtype)
+    whole = lax.dynamic_update_slice_in_dim(whole, array, index * extent, axis=dim)
+    from_left = from_right = array
+    middle = size // 2
+    for turn in range(1, middle + 1):
+        from_left = lax.ppermute(from_left, axis, ahead)
+        whole = lax.dynamic_update_slice_in_dim(
+            whole, from_left, (index - turn) % size * extent, axis=dim
+        )
+        if turn < size - middle:
+            from_right = lax.ppermute(from_right, axis, left)
+            whole = lax.dynamic_update_slice_in_dim(
+                whole, from_right, (index + turn) % size * extent, axis=dim
+            )
+    return whole
 
 
 def lower_diff(field):
@@ -76,7 +97,7 @@
     ).astype(jnp.float32)
     full_one, full_two, full_three = (
         lax.all_gather(weight_one, "slab", axis=0, tiled=True),
-        lax.all_gather(weight_two, "slab", axis=0, tiled=True),
+        gather_around(weight_two, "slab", 0),
         lax.all_gather(weight_three, "slab", axis=0, tiled=True),
     )
     forward_part = jnp.take(forward_raw, inverse, axis=1)

time: 541 us -> 565 us (1.044)
  starting transfers between devices: 20.7 us -> 46.8 us
  blocking collectives: 61.4 us -> 39.1 us
  local copies, waits for them, and re-layouts: 177 us -> 190 us
    ppermute x0 -> x15, starting transfers between devices: none -> 32.2 us  [the longest x7 31.1 us: gather_around(): from_right = lax.ppermute(from_right, axis, left)]
    all_gather x1 -> x0, blocking collectives: 20.3 us -> none  [body(): lax.all_gather(weight_two, 'slab', axis=0, tiled=True)]
    dynamic_update_slice x0 -> x16, local copies, waits for them, and re-layouts: none -> 11.9 us  [the longest x8 6.35 us: gather_around(): lax.dynamic_update_slice_in_dim(whole, from_left, (index - turn) % size *...]
    ppermute x0 -> x15, waiting for transfers between devices: none -> 6.5 us  [the longest x8 6.48 us: gather_around(): from_left = lax.ppermute(from_left, axis, ahead)]
    unnamed x44 -> x46, local copies, waits for them, and re-layouts: 23.4 us -> 23.4 us
  transfers between devices with their start and end apart: 7 -> 22, of which waited for: 5 -> 10; matrix products, arithmetic and copies ran while one was open for 11% -> 47% of each run, Pallas kernels for 0% -> 0%
where the time goes in v1:
time: 565 us; the launch traced here: 564 us
  waiting for transfers between devices  192 us (34%)
  local copies, waits for them, and re-layouts  190 us (34%)
  other arithmetic  72.5 us (13%)
  starting transfers between devices  46.8 us (8%)
  blocking collectives  39.1 us (7%)
  between operations  15.3 us (3%)
  matrix products  7.3 us (1%)
    unnamed x5, waiting for transfers between devices  114 us
    unnamed x3, other arithmetic  63.6 us
    reduce_scatter x1, waiting for transfers between devices, body(): lax.psum_scatter(local_two, 'slab', scatter_dimension=0, tiled=True)  61.9 us
    gather x1, local copies, waits for them, and re-layouts, body(): south = jnp.take(horizontal_wind[1], neighbors[3], axis=1)  34.3 us
    gather x1, local copies, waits for them, and re-layouts, body(): east = jnp.take(horizontal_wind[0], neighbors[0], axis=1)  34.3 us
    gather x1, local copies, waits for them, and re-layouts, body(): west = jnp.take(horizontal_wind[0], neighbors[1], axis=1)  34.3 us
    gather x1, local copies, waits for them, and re-layouts, body(): north = jnp.take(horizontal_wind[1], neighbors[2], axis=1)  34.3 us
    ppermute x7, starting transfers between devices, gather_around(): from_right = lax.ppermute(from_right, axis, left)  31.1 us
  transfers between devices with their start and end apart: 22, of which 10 were waited for; matrix products, arithmetic and copies ran while one was open for 47% of the time, Pallas kernels for 0%

profile of v1, /device:TPU:0, one launch (start us, length us, event | category | flops | bytes accessed | tf_op | source)
XLA Modules:
  0.0 563.7 jit_solution(7772306475349371403)
XLA Ops:
  7.7 5.0 collective-permute-start.1
  12.7 1.2 fusion.39
  13.9 0.8 fusion.40
  14.7 34.3 %gather_fusion.4 = f32[6144]{0:T(1024)S(1)} fusion(f32[6144]{0:T(1024)S(1)} %bitcast.146, s32[6144]{0:T(1024)S(1)} %fusion.24), kind=kCustom, calls=%fused_computation.3.clone | custom fusion | bytes 73728 | tf_op jit(solution)/shard_map/jit(_take)/gather | solution.py:85
  49.0 34.3 %gather_fusion.5 = f32[6144]{0:T(1024)S(1)} fusion(f32[6144]{0:T(1024)S(1)} %bitcast.147, s32[6144]{0:T(1024)S(1)} %fusion.25), kind=kCustom, calls=%fused_computation.4.clone | custom fusion | bytes 73728 | tf_op jit(solution)/shard_map/jit(_take)/gather | solution.py:86
  83.3 34.3 %gather_fusion.2 = f32[6144]{0:T(1024)S(1)} fusion(f32[6144]{0:T(1024)S(1)} %bitcast.144, s32[6144]{0:T(1024)S(1)} %fusion.22), kind=kCustom, calls=%fused_computation.clone | custom fusion | bytes 73728 | tf_op jit(solution)/shard_map/jit(_take)/gather | solution.py:83
  117.7 34.3 %gather_fusion.3 = f32[6144]{0:T(1024)S(1)} fusion(f32[6144]{0:T(1024)S(1)} %bitcast.145, s32[6144]{0:T(1024)S(1)} %fusion.23), kind=kCustom, calls=%fused_computation.2.clone | custom fusion | bytes 73728 | tf_op jit(solution)/shard_map/jit(_take)/gather | solution.py:84
  152.4 4.0 copy.60
  157.0 34.5 %reduce.6 = bf16[6144,4]{1,0:T(8,128)(2,1)} reduce(bf16[6144,1,4]{2,1,0:T(2,128)(2,1)S(1)} %bitcast.148, bf16[]{:T(256)} %broadcast.263), dimensions={1}, to_apply=%bitcast.113.reduce_sub_computation | reduce | bytes 98306
  191.6 4.4 reshape.350
  195.9 3.7 all-to-all-start
  199.9 1.2 sort.17
  202.5 1.4 cholesky.17
  204.0 0.6 compare_reduce_fusion
  204.7 0.6 fusion.27
  205.3 1.2 custom-call.10
  206.9 0.8 broadcast_in_dim.113
  207.7 0.6 constant_dynamic-update-slice_fusion.15
  208.4 21.5 %all-gather = bf16[16,4,512]{2,1,0:T(4,128)(2,1)S(1)} all-gather(bf16[1,4,512]{2,1,0:T(4,128)(2,1)S(1)} %bitcast.174), channel_id=1, replica_groups=mesh['date'=2,'slab'=16] {'slab'}, dimensions={0}, use_global_device_ids=true | all-gather | bytes 69632 | tf_op jit(solution)/shard_map/all_gather | solution.py:99
  229.9 17.6 %all-gather.1 = bf16[16,32,16]{1,2,0:T(8,128)(2,1)S(1)} all-gather(bf16[1,32,16]{1,2,0:T(8,128)(2,1)S(1)} %bitcast.175), channel_id=1, replica_groups=mesh['date'=2,'slab'=16] {'slab'}, dimensions={0}, use_global_device_ids=true | all-gather | bytes 17408 | tf_op jit(solution)/shard_map/all_gather | solution.py:101
  247.7 3.3 copy.66
  251.5 28.4 %reduce.7 = f32[6144,2]{1,0:T(8,128)} reduce(f32[6144,1,2]{2,1,0:T(1,128)S(1)} %bitcast.149, f32[]{:T(128)} %broadcast.264), dimensions={1}, to_apply=%bitcast.115.reduce_sub_computation | reduce | bytes 98308
  279.9 4.3 reshape.352
  284.6 4.1 collective-permute-start.3
  290.4 4.4 collective-permute-start.5
  294.8 1.4 constant_dynamic-update-slice_fusion.12
  296.8 3.5 all-to-all-start.2
  300.5 4.0 reshape.351
  304.5 2.9 copy.61
  307.5 0.6 gather_fusion
  308.2 0.8 reduce.8
  309.0 4.5 reshape.353
  313.6 1.2 copy.68
  314.7 0.6 gather_fusion.7
  316.2 4.2 collective-permute-start.7
  320.4 1.4 constant_dynamic-update-slice_fusion.10
  321.7 1.4 constant_dynamic-update-slice_fusion.9
  323.1 4.4 collective-permute-start.9
  327.5 0.6 constant_dynamic-update-slice_fusion.8
  329.2 4.4 collective-permute-start.11
  335.2 4.4 collective-permute-start.13
  339.6 0.6 constant_dynamic-update-slice_fusion.4
  340.2 0.6 constant_dynamic-update-slice_fusion.3
  342.4 4.8 collective-permute-done.14
  347.9 1.5 convolution_tanh_fusion
  350.5 0.8 copy.77
  351.5 1.5 fusion
  352.9 0.8 convolution_multiply_fusion.2
  353.8 1.5 convolution_multiply_fusion
  356.3 0.7 reduce.9
  357.1 0.7 reshape.354
  357.8 3.5 all-to-all-start.3
  361.3 0.6 gather_fusion.6
  361.9 0.7 bitcast_convert_fusion
  362.6 5.1 all-to-all-done.3
  367.7 3.5 all-to-all-start.1
  372.6 0.6 convert.23
  373.2 4.5 all-to-all-done.1
  377.8 0.7 fusion.41
  378.4 26.0 %reduce-scatter.7.cloned.1.call-done = f32[32,16]{1,0:T(8,128)} async-done(((f32[512,16]{1,0:T(8,128)}), f32[32,16]{1,0:T(8,128)}) %reduce-scatter.7.cloned.1.call-update) | async-done | bytes 2064
  404.4 1.4 copy.78
  405.8 88.1 %all-reduce.6.cloned.1.call-done = f32[64,512]{1,0:T(8,128)} async-done(((f32[64,512]{1,0:T(8,128)}), f32[64,512]{1,0:T(8,128)}) %all-reduce.6.cloned.1.call-update) | async-done | bytes 131088
  493.9 1.3 constant_dynamic-slice_fusion
  495.2 61.9 %reduce-scatter.5.cloned.1.call-done = f32[32,512]{1,0:T(8,128)} async-done(((f32[512,512]{1,0:T(8,128)}), f32[32,512]{1,0:T(8,128)}) %reduce-scatter.5.cloned.1.call-update) | async-done | bytes 65552 | tf_op jit(solution)/shard_map/reduce_scatter | solution.py:144
  (129 shorter events, 15.5 us)
Async XLA Ops:
  7.2 277.0 %collective-permute-start = (bf16[32,512]{1,0:T(8,128)(2,1)}, bf16[32,512]{1,0:T(8,128)(2,1)S(1)}, u32[]{:S(2)}, u32[]{:S(2)}) collective-permute-start(bf16[32,512]{1,0:T(8,128)(2,1)} %param.28), channel_id=1, source_target_pairs={{0,1},{1,2},{2,3},{3,4},{4,5},{5,6},{6,7},{7,8},{8,9},{9,10},{10,1... | collective-permute-start | bytes 98312 | tf_op jit(solution)/shard_map/ppermute | solution.py:17
  7.7 276.9 %collective-permute-start.1 = (bf16[32,512]{1,0:T(8,128)(2,1)}, bf16[32,512]{1,0:T(8,128)(2,1)S(1)}, u32[]{:S(2)}, u32[]{:S(2)}) collective-permute-start(bf16[32,512]{1,0:T(8,128)(2,1)} %param.28), channel_id=1, source_target_pairs={{0,15},{1,0},{2,1},{3,2},{4,3},{5,4},{6,5},{7,6},{8,7},{9,8},{10,9... | collective-permute-start | bytes 98312 | tf_op jit(solution)/shard_map/ppermute | solution.py:22
  117.6 34.4 %copy-start.3 = (f32[1,6144]{1,0:T(1,128)S(1)}, f32[1,6144]{1,0:T(1,128)}, u32[]{:S(2)}) copy-start(f32[1,6144]{1,0:T(1,128)} %param.19) | copy-start | bytes 73732
  117.7 34.4 %copy-start = (f32[2,6144]{1,0:T(2,128)S(1)}, f32[2,6144]{1,0:T(2,128)}, u32[]{:S(2)}) copy-start(f32[2,6144]{1,0:T(2,128)} %param.22) | copy-start | bytes 147460
  117.7 34.4 %copy-start.2 = (f32[1,6144]{1,0:T(1,128)S(1)}, f32[1,6144]{1,0:T(1,128)}, u32[]{:S(2)}) copy-start(f32[1,6144]{1,0:T(1,128)} %param.18) | copy-start | bytes 73732
  117.7 34.5 %copy-start.4 = (f32[1,6144]{1,0:T(1,128)S(1)}, f32[1,6144]{1,0:T(1,128)}, u32[]{:S(2)}) copy-start(f32[1,6144]{1,0:T(1,128)} %param.20) | copy-start | bytes 73732
  157.0 43.0 %copy-start.14 = (s32[16]{0:T(128)S(1)}, s32[16]{0:T(128)}, u32[]{:S(2)}) copy-start(s32[16]{0:T(128)} %param.24) | copy-start | bytes 196
  157.0 45.4 %copy-start.10 = (f32[16]{0:T(128)S(1)}, f32[16]{0:T(128)}, u32[]{:S(2)}) copy-start(f32[16]{0:T(128)} %param.25) | copy-start | bytes 196
  157.0 45.4 %copy-start.13 = (pred[16]{0:T(512)(128)(4,1)S(1)}, pred[16]{0:T(512)(128)(4,1)}, u32[]{:S(2)}) copy-start(pred[16]{0:T(512)(128)(4,1)} %constant.205.clone.1) | copy-start | bytes 52
  157.0 50.7 %copy-start.1 = (bf16[32,512]{1,0:T(8,128)(2,1)S(1)}, bf16[32,512]{1,0:T(8,128)(2,1)}, u32[]{:S(2)}) copy-start(bf16[32,512]{1,0:T(8,128)(2,1)} %param.28) | copy-start | bytes 98308
  157.0 51.3 %copy-start.5 = (f32[1,6144]{1,0:T(1,128)S(1)}, f32[1,6144]{1,0:T(1,128)}, u32[]{:S(2)}) copy-start(f32[1,6144]{1,0:T(1,128)} %param.31) | copy-start | bytes 73732
  157.0 51.3 %copy-start.6 = (f32[1,6144]{1,0:T(1,128)S(1)}, f32[1,6144]{1,0:T(1,128)}, u32[]{:S(2)}) copy-start(f32[1,6144]{1,0:T(1,128)} %param.30) | copy-start | bytes 73732
  157.0 51.4 %copy-start.7 = (bf16[4,512]{1,0:T(4,128)(2,1)S(1)}, bf16[4,512]{1,0:T(4,128)(2,1)}, u32[]{:S(2)}) copy-start(bf16[4,512]{1,0:T(4,128)(2,1)} %param.27) | copy-start | bytes 12292
  157.0 72.9 %copy-start.8 = (bf16[32,16]{0,1:T(8,128)(2,1)S(1)}, bf16[32,16]{0,1:T(8,128)(2,1)}, u32[]{:S(2)}) copy-start(bf16[32,16]{0,1:T(8,128)(2,1)} %param.29) | copy-start | bytes 3076
  195.9 100.8 %all-to-all-start = ((bf16[16,2,768]{2,1,0:T(2,128)(2,1)}), bf16[16,2,768]{2,1,0:T(2,128)(2,1)S(1)}, u32[]{:S(2)}, u32[]{:S(2)}) async-start(bf16[16,2,768]{2,1,0:T(2,128)(2,1)} %reshape.350), calls=%async_computation | async-start | bytes 98304 | tf_op jit(solution)/shard_map/all_to_all | solution.py:91
  284.2 6.1 %collective-permute-start.2 = (bf16[32,512]{1,0:T(8,128)(2,1)S(1)}, bf16[32,512]{1,0:T(8,128)(2,1)}, u32[]{:S(2)}, u32[]{:S(2)}) collective-permute-start(bf16[32,512]{1,0:T(8,128)(2,1)S(1)} %collective-permute-done), channel_id=1, source_target_pairs={{0,1},{1,2},{2,3},{3,4},{4,5},{5,6},{6,7},{7,8},{8,9},{9,10},{10,1... | collective-permute-start | bytes 98312 | tf_op jit(solution)/shard_map/ppermute | solution.py:17
  284.6 5.8 %collective-permute-start.3 = (bf16[32,512]{1,0:T(8,128)(2,1)S(1)}, bf16[32,512]{1,0:T(8,128)(2,1)S(1)}, u32[]{:S(2)}, u32[]{:S(2)}) collective-permute-start(bf16[32,512]{1,0:T(8,128)(2,1)S(1)} %collective-permute-done.1), channel_id=1, source_target_pairs={{0,15},{1,0},{2,1},{3,2},{4,3},{5,4},{6,5},{7,6},{8,7},{9,8},{10,9... | collective-permute-start | bytes 98312 | tf_op jit(solution)/shard_map/ppermute | solution.py:22
  290.4 25.5 %collective-permute-start.4 = (bf16[32,512]{1,0:T(8,128)(2,1)}, bf16[32,512]{1,0:T(8,128)(2,1)}, u32[]{:S(2)}, u32[]{:S(2)}) collective-permute-start(bf16[32,512]{1,0:T(8,128)(2,1)} %collective-permute-done.2), channel_id=1, source_target_pairs={{0,1},{1,2},{2,3},{3,4},{4,5},{5,6},{6,7},{7,8},{8,9},{9,10},{10,1... | collective-permute-start | bytes 98312 | tf_op jit(solution)/shard_map/ppermute | solution.py:17
  290.4 25.8 %collective-permute-start.5 = (bf16[32,512]{1,0:T(8,128)(2,1)S(1)}, bf16[32,512]{1,0:T(8,128)(2,1)}, u32[]{:S(2)}, u32[]{:S(2)}) collective-permute-start(bf16[32,512]{1,0:T(8,128)(2,1)S(1)} %collective-permute-done.3), channel_id=1, source_target_pairs={{0,15},{1,0},{2,1},{3,2},{4,3},{5,4},{6,5},{7,6},{8,7},{9,8},{10,9... | collective-permute-start | bytes 98312 | tf_op jit(solution)/shard_map/ppermute | solution.py:22
  296.8 11.4 %all-to-all-start.2 = ((f32[16,1,768]{2,1,0:T(1,128)}), f32[16,1,768]{2,1,0:T(1,128)S(1)}, u32[]{:S(2)}, u32[]{:S(2)}) async-start(f32[16,1,768]{2,1,0:T(1,128)} %reshape.352), calls=%async_computation.2 | async-start | bytes 98304 | tf_op jit(solution)/shard_map/all_to_all | solution.py:127
  300.3 104.1 %reduce-scatter.7.cloned.1.call-start = ((), (), s32[]{:S(2)}) async-start(), calls=%async_computation.7 | async-start | bytes 278528
  313.5 1.9 copy-start.12
  313.5 35.8 %copy-start.11 = (f32[16]{0:T(128)S(1)}, f32[16]{0:T(128)}, u32[]{:S(2)}) copy-start(f32[16]{0:T(128)} %param.26) | copy-start | bytes 196
  315.9 7.2 %collective-permute-start.6 = (bf16[32,512]{1,0:T(8,128)(2,1)}, bf16[32,512]{1,0:T(8,128)(2,1)S(1)}, u32[]{:S(2)}, u32[]{:S(2)}) collective-permute-start(bf16[32,512]{1,0:T(8,128)(2,1)} %collective-permute-done.4), channel_id=1, source_target_pairs={{0,1},{1,2},{2,3},{3,4},{4,5},{5,6},{6,7},{7,8},{8,9},{9,10},{10,1... | collective-permute-start | bytes 98312 | tf_op jit(solution)/shard_map/ppermute | solution.py:17
  316.2 6.9 %collective-permute-start.7 = (bf16[32,512]{1,0:T(8,128)(2,1)}, bf16[32,512]{1,0:T(8,128)(2,1)S(1)}, u32[]{:S(2)}, u32[]{:S(2)}) collective-permute-start(bf16[32,512]{1,0:T(8,128)(2,1)} %collective-permute-done.5), channel_id=1, source_target_pairs={{0,15},{1,0},{2,1},{3,2},{4,3},{5,4},{6,5},{7,6},{8,7},{9,8},{10,9... | collective-permute-start | bytes 98312 | tf_op jit(solution)/shard_map/ppermute | solution.py:22
  323.1 6.1 %collective-permute-start.8 = (bf16[32,512]{1,0:T(8,128)(2,1)S(1)}, bf16[32,512]{1,0:T(8,128)(2,1)S(1)}, u32[]{:S(2)}, u32[]{:S(2)}) collective-permute-start(bf16[32,512]{1,0:T(8,128)(2,1)S(1)} %collective-permute-done.6), channel_id=1, source_target_pairs={{0,1},{1,2},{2,3},{3,4},{4,5},{5,6},{6,7},{7,8},{8,9},{9,10},{10,1... | collective-permute-start | bytes 98312 | tf_op jit(solution)/shard_map/ppermute | solution.py:17
  323.1 6.1 %collective-permute-start.9 = (bf16[32,512]{1,0:T(8,128)(2,1)S(1)}, bf16[32,512]{1,0:T(8,128)(2,1)S(1)}, u32[]{:S(2)}, u32[]{:S(2)}) collective-permute-start(bf16[32,512]{1,0:T(8,128)(2,1)S(1)} %collective-permute-done.7), channel_id=1, source_target_pairs={{0,15},{1,0},{2,1},{3,2},{4,3},{5,4},{6,5},{7,6},{8,7},{9,8},{10,9... | collective-permute-start | bytes 98312 | tf_op jit(solution)/shard_map/ppermute | solution.py:22
  329.1 6.0 %collective-permute-start.10 = (bf16[32,512]{1,0:T(8,128)(2,1)S(1)}, bf16[32,512]{1,0:T(8,128)(2,1)S(1)}, u32[]{:S(2)}, u32[]{:S(2)}) collective-permute-start(bf16[32,512]{1,0:T(8,128)(2,1)S(1)} %collective-permute-done.8), channel_id=1, source_target_pairs={{0,1},{1,2},{2,3},{3,4},{4,5},{5,6},{6,7},{7,8},{8,9},{9,10},{10,1... | collective-permute-start | bytes 98312 | tf_op jit(solution)/shard_map/ppermute | solution.py:17
  329.2 6.0 %collective-permute-start.11 = (bf16[32,512]{1,0:T(8,128)(2,1)S(1)}, bf16[32,512]{1,0:T(8,128)(2,1)S(1)}, u32[]{:S(2)}, u32[]{:S(2)}) collective-permute-start(bf16[32,512]{1,0:T(8,128)(2,1)S(1)} %collective-permute-done.9), channel_id=1, source_target_pairs={{0,15},{1,0},{2,1},{3,2},{4,3},{5,4},{6,5},{7,6},{8,7},{9,8},{10,9... | collective-permute-start | bytes 98312 | tf_op jit(solution)/shard_map/ppermute | solution.py:22
  335.2 6.0 %collective-permute-start.12 = (bf16[32,512]{1,0:T(8,128)(2,1)S(1)}, bf16[32,512]{1,0:T(8,128)(2,1)S(1)}, u32[]{:S(2)}, u32[]{:S(2)}) collective-permute-start(bf16[32,512]{1,0:T(8,128)(2,1)S(1)} %collective-permute-done.10), channel_id=1, source_target_pairs={{0,1},{1,2},{2,3},{3,4},{4,5},{5,6},{6,7},{7,8},{8,9},{9,10},{10,1... | collective-permute-start | bytes 98312 | tf_op jit(solution)/shard_map/ppermute | solution.py:17
  335.2 6.6 %collective-permute-start.13 = (bf16[32,512]{1,0:T(8,128)(2,1)S(1)}, bf16[32,512]{1,0:T(8,128)(2,1)S(1)}, u32[]{:S(2)}, u32[]{:S(2)}) collective-permute-start(bf16[32,512]{1,0:T(8,128)(2,1)S(1)} %collective-permute-done.11), channel_id=1, source_target_pairs={{0,15},{1,0},{2,1},{3,2},{4,3},{5,4},{6,5},{7,6},{8,7},{9,8},{10,9... | collective-permute-start | bytes 98312 | tf_op jit(solution)/shard_map/ppermute | solution.py:22
  341.2 6.0 %collective-permute-start.14 = (bf16[32,512]{1,0:T(8,128)(2,1)S(1)}, bf16[32,512]{1,0:T(8,128)(2,1)S(1)}, u32[]{:S(2)}, u32[]{:S(2)}) collective-permute-start(bf16[32,512]{1,0:T(8,128)(2,1)S(1)} %collective-permute-done.12), channel_id=1, source_target_pairs={{0,1},{1,2},{2,3},{3,4},{4,5},{5,6},{6,7},{7,8},{8,9},{9,10},{10,1... | collective-permute-start | bytes 98312 | tf_op jit(solution)/shard_map/ppermute | solution.py:17
  351.4 4.8 copy-start.9
  351.4 142.5 %all-reduce.6.cloned.1.call-start = ((), (), s32[]{:S(2)}) async-start(), calls=%async_computation.8 | async-start | bytes 262144
  352.9 18.3 %copy-start.15 = (u32[32]{0:T(128)S(1)}, u32[32]{0:T(128)}, u32[]{:S(2)}) copy-start(u32[32]{0:T(128)} %constant.242) | copy-start | bytes 388
  353.8 203.4 %reduce-scatter.5.cloned.1.call-start = ((), (), s32[]{:S(2)}) async-start(), calls=%async_computation.6 | async-start | bytes 1114112 | tf_op jit(solution)/shard_map/reduce_scatter | solution.py:144
  357.8 10.0 %all-to-all-start.3 = ((bf16[16,2,192]{2,1,0:T(2,128)(2,1)}), bf16[16,2,192]{2,1,0:T(2,128)(2,1)S(1)}, u32[]{:S(2)}, u32[]{:S(2)}) async-start(bf16[16,2,192]{2,1,0:T(2,128)(2,1)} %reshape.354), calls=%async_computation.3 | async-start | bytes 32768 | tf_op jit(solution)/shard_map/all_to_all | solution.py:152
  367.7 10.0 %all-to-all-start.1 = ((bf16[2,16,384]{2,0,1:T(2,128)(2,1)}), bf16[2,16,384]{2,0,1:T(2,128)(2,1)S(1)}, u32[]{:S(2)}, u32[]{:S(2)}) async-start(bf16[2,16,384]{2,0,1:T(2,128)(2,1)} %bitcast_convert_fusion), calls=%async_computation.1 | async-start | bytes 49152 | tf_op jit(solution)/shard_map/all_to_all | solution.py:120
Sparse Core Ops, SparseCore 0:
  351.5 52.8 reduce-scatter.6
  407.9 85.9 all-reduce.5
  498.1 59.0 reduce-scatter.4
